TPU v7x, 768 devices: a whole 4x8x12 slice. The times are simulated.
768 devices in a mesh: blk: 16 (over y, z_hi), dev: 48 (over x, z_lo, core).
Axes of the slice: x: 4, y: 8, z: 12 (z_hi: 2, z_lo: 6; z = z_hi * 6 + z_lo), core: 2. Of those that a mesh axis runs over, the one named last changes fastest.
Arguments:
- factors: bfloat16 [393216, 128], P(('blk', 'dev')), may hold values from -3 to 3
- item_factors: bfloat16 [2048, 128], P('blk')
- block_values: bfloat16 [73728, 128, 128], P(('blk', 'dev')), may hold values from 0 to 8, as said below
- block_rows: int32 [73728], P(('blk', 'dev')), may hold values from 0 to 191, as said below
- block_cols: int32 [73728], P(('blk', 'dev')), may hold values from -1 to 15, as said below
- row_place: int32 [16, 192], P('blk'), may hold values from 0 to 191, as said below
Outputs:
- solution: float32 [393216, 128], P(('blk', 'dev'))
- residual: float32 [393216, 128], P(('blk', 'dev'))
Inputs may be any that keep to these rules, and one draw needn't show every extreme that they name: `row_place`: each row of the table is a permutation of 0 to 191: user block row g of the group is held by the device value // 4 of dev, at block position value % 4. `block_rows`: slots 2 o and 2 o + 1 of a device's list hold blocks of user block rows held by device o of dev in the same blk group, whether live or not. `block_cols`: empty slots are marked -1 and their values are to be ignored. Of the two slots that one device holds for one holder device, at most one is live. No two live blocks share both user block row and item block. Of the slots bound for one holder device, at most 3 live ones fall on one item block, and in every blk group some device receives exactly 3 live blocks on every item block. `block_values`: entries are zero or between 0.5 and 8.
All inputs are finite; a program needn't handle non-finite values.
Results may differ from a plain program's by a relative error of at most 0.0054.
Values may be sent and summed in bfloat16 or wider, within the bound.
No kernel may reach another device: no remote copies, remote signals or barrier semaphores. Data moves between devices by JAX's collectives and lax.ppermute only.
A program may use at most 32 MiB of HBM per device.

v0:
```python
import jax
import jax.numpy as jnp
from jax import lax
from jax.sharding import PartitionSpec as P

ITERS = 2


ridge_weight = 0.5
epsilon = 1e-06


def body(factors, item_factors, block_values, block_rows, block_cols, row_place):
    dev_count = lax.axis_size("dev")
    group_count = lax.axis_size("blk")
    per_panel = dev_count // group_count
    block_edge = block_values.shape[1]
    rank_width = factors.shape[1]
    user_blocks = factors.shape[0] // block_edge
    paired_values = block_values.reshape(dev_count, 2, block_edge, block_edge)
    paired_rows = block_rows.reshape(dev_count, 2)
    paired_cols = block_cols.reshape(dev_count, 2)
    second_live = paired_cols[:, 1] >= 0
    picked_values = jnp.where(second_live[:, None, None], paired_values[:, 1], paired_values[:, 0])
    picked_rows = jnp.where(second_live, paired_rows[:, 1], paired_rows[:, 0])
    picked_cols = jnp.where(second_live, paired_cols[:, 1], paired_cols[:, 0])
    received, holder_rows, item_blocks = (
        lax.all_to_all(picked_values, "dev", split_axis=0, concat_axis=0, tiled=True),
        lax.all_to_all(picked_rows, "dev", split_axis=0, concat_axis=0, tiled=True),
        lax.all_to_all(picked_cols, "dev", split_axis=0, concat_axis=0, tiled=True),
    )
    slot_count = item_blocks.shape[0]
    positions = jnp.take(row_place[0], holder_rows) % user_blocks
    panel_key = jnp.where(item_blocks >= 0, item_blocks, group_count)
    ranking = jnp.argsort(panel_key, stable=True)
    matches = panel_key[None, :] == jnp.arange(group_count, dtype=jnp.int32)[:, None]
    counts = jnp.sum(matches.astype(jnp.int32), axis=1)
    offsets = jnp.cumsum(counts) - counts
    column_ids = jnp.arange(per_panel, dtype=jnp.int32)
    filled = column_ids[None, :] < counts[:, None]
    chosen = ranking[jnp.minimum(offsets[:, None] + column_ids[None, :], slot_count - 1)]
    weights = jnp.where(filled[:, :, None, None], received[chosen], jnp.zeros((), jnp.bfloat16))
    confidence = jnp.where(weights > 0, 1.0 + weights.astype(jnp.float32), 0.0).astype(jnp.bfloat16)
    holder_pos = positions[chosen]
    scatter_table = (
        holder_pos[:, :, None] == jnp.arange(user_blocks, dtype=holder_pos.dtype)[None, None, :]
    ).astype(jnp.float32)

    def block_products(direction, panel_rows, with_rhs):
        row_count = panel_rows.shape[0]
        panel_span = max(row_count // block_edge, 1)
        item_rows = panel_rows.reshape(panel_span, row_count // panel_span, rank_width)
        user_rows = direction[holder_pos]
        scores = jnp.einsum(
            "kpur,kir->kpui", user_rows, item_rows, preferred_element_type=jnp.float32
        )
        scaled = (scores * weights).astype(jnp.bfloat16)
        carried = jnp.einsum(
            "kpui,kir->kpur", scaled, item_rows, preferred_element_type=jnp.float32
        )
        block_sum = jnp.einsum(
            "kpb,kpur->bur", scatter_table, carried, precision=lax.Precision.HIGHEST
        )
        if with_rhs:
            lifted = jnp.einsum(
                "kpui,kir->kpur", confidence, item_rows, preferred_element_type=jnp.float32
            )
            rhs_sum = jnp.einsum(
                "kpb,kpur->bur", scatter_table, lifted, precision=lax.Precision.HIGHEST
            )
            return (block_sum, rhs_sum)
        return block_sum

    def visit_panels(step_fn, initial):
        return step_fn(
            initial, lax.all_gather(item_factors, "blk", axis=0, tiled=True), jnp.int32(0)
        )

    start_direction = factors.reshape(user_blocks, block_edge, rank_width)

    def first_pass(totals, panel_rows, first_row):
        block_sum, rhs_sum = block_products(start_direction, panel_rows, True)
        result = (block_sum, rhs_sum)
        return result

    def later_pass(direction):

        def fold_step(totals, panel_rows, first_row):
            return block_products(direction, panel_rows, False)

        return fold_step

    empty_users = jnp.zeros((user_blocks, block_edge, rank_width), jnp.float32)
    first_term, right_side = visit_panels(first_pass, (empty_users, empty_users))
    local_gram = jnp.dot(item_factors.T, item_factors, preferred_element_type=jnp.float32)
    gram_matrix = lax.psum(local_gram, "blk")

    def operator_rest(vector, block_sum):
        return (
            block_sum.reshape(-1, rank_width)
            + jnp.dot(vector, gram_matrix, precision=lax.Precision.HIGHEST)
            + ridge_weight * vector
        )

    solution = factors.astype(jnp.float32)
    residual = right_side.reshape(-1, rank_width) - operator_rest(solution, first_term)
    direction = residual
    norm_now = jnp.sum(residual * residual, axis=1)
    for sweep_index in range(ITERS):
        direction_rows = direction.astype(jnp.bfloat16).reshape(user_blocks, block_edge, rank_width)
        block_sum = visit_panels(later_pass(direction_rows), empty_users)
        image = operator_rest(direction, block_sum)
        curvature = jnp.sum(direction * image, axis=1)
        step_length = norm_now / (curvature + epsilon)
        solution = solution + step_length[:, None] * direction
        residual = residual - step_length[:, None] * image
        if sweep_index + 1 < ITERS:
            norm_next = jnp.sum(residual * residual, axis=1)
            direction = residual + (norm_next / (norm_now + epsilon))[:, None] * direction
            norm_now = norm_next
    return (solution, residual)


def solution(mesh):
    return jax.shard_map(
        body,
        mesh=mesh,
        in_specs=(
            P(("blk", "dev"), None),
            P("blk", None),
            P(("blk", "dev"), None, None),
            P(("blk", "dev")),
            P(("blk", "dev")),
            P("blk", None),
        ),
        out_specs=(P(("blk", "dev"), None), P(("blk", "dev"), None)),
        check_vma=False,
    )
```

profile of v0, /device:TPU:2, one launch (start us, length us, event | category | flops | bytes accessed | tf_op | source)
XLA Modules:
  0.0 361.8 jit_solution(2244942085666669882)
XLA Ops:
  7.2 0.8 reshape.272
  8.0 0.2 slice_reduce_fusion.3
  8.1 0.8 reshape.273
  8.9 0.2 slice_reduce_fusion.2
  9.1 0.7 copy.87
  9.8 15.5 %all-to-all-start = ((s32[48,1,1]{2,1,0:T(1,128)}), s32[48,1,1]{2,1,0:T(1,128)S(1)}, u32[]{:S(2)}, u32[]{:S(2)}) async-start(s32[48,1,1]{2,1,0:T(1,128)} %copy.87), calls=%async_computation | async-start | bytes 49152 | tf_op jit(solution)/shard_map/all_to_all | solution.py:29
  25.3 0.2 compare_reduce_fusion
  25.5 0.7 copy.91
  26.2 8.6 %all-to-all-done = s32[48,1,1]{2,1,0:T(1,128)S(1)} async-done(((s32[48,1,1]{2,1,0:T(1,128)}), s32[48,1,1]{2,1,0:T(1,128)S(1)}, u32[]{:S(2)}, u32[]{:S(2)}) %all-to-all-start) | async-done | bytes 224 | tf_op jit(solution)/shard_map/all_to_all | solution.py:29
  34.8 5.5 %all-to-all-start.1 = ((s32[48,1,1]{2,1,0:T(1,128)}), s32[48,1,1]{2,1,0:T(1,128)S(1)}, u32[]{:S(2)}, u32[]{:S(2)}) async-start(s32[48,1,1]{2,1,0:T(1,128)} %copy.91), calls=%async_computation.1 | async-start | bytes 49152 | tf_op jit(solution)/shard_map/all_to_all | solution.py:30
  40.3 3.3 fusion.11
  43.5 6.2 %all-to-all-done.1 = s32[48,1,1]{2,1,0:T(1,128)S(1)} async-done(((s32[48,1,1]{2,1,0:T(1,128)}), s32[48,1,1]{2,1,0:T(1,128)S(1)}, u32[]{:S(2)}, u32[]{:S(2)}) %all-to-all-start.1) | async-done | bytes 224 | tf_op jit(solution)/shard_map/all_to_all | solution.py:30
  49.8 6.3 %all-to-all-start.2 = ((bf16[48,128,128]{2,1,0:T(8,128)(2,1)}), bf16[48,128,128]{2,1,0:T(8,128)(2,1)}, u32[]{:S(2)}, u32[]{:S(2)}) async-start(bf16[48,128,128]{2,1,0:T(8,128)(2,1)} %fusion.11), calls=%async_computation.2 | async-start | bytes 3145728 | tf_op jit(solution)/shard_map/all_to_all | solution.py:28
  56.2 0.8 fusion.50
  57.0 0.1 copy.86
  57.1 95.8 %all_gather.2 = bf16[2048,128]{1,0:T(8,128)(2,1)S(1)} all-gather(bf16[128,128]{1,0:T(8,128)(2,1)S(1)} %copy-done.4), channel_id=1, replica_groups=mesh['blk'=16,'dev'=48] {'blk'}, dimensions={0}, use_global_device_ids=true | all-gather | bytes 557056 | tf_op jit(solution)/shard_map/all_gather | solution.py:76
  152.9 0.9 reduce.6
  153.9 2.0 sort.17
  156.2 0.1 reduce.7
  156.5 0.8 gather_fusion.1
  157.6 0.8 gather_fusion
  158.4 0.9 reduce.3
  159.4 0.8 gather_fusion.2
  160.5 1.9 gather_fusion.4
  162.5 2.3 gather_fusion.3
  164.8 2.3 fusion.9
  167.1 4.1 %fusion.16 = f32[16,3,128,128]{3,2,1,0:T(8,128)} fusion(bf16[16,128,128,1]{2,1,3,0:T(8,128)(2,1)S(1)} %bitcast.100, bf16[16,3,128,128]{3,2,1,0:T(8,128)(2,1)} %bitcast.109, bf16[16,3,128,128]{3,2,1,0:T(8,128)(2,1)S(1)} %bitcast.104, pred[16,3]{1,0:T(8,128)(4,1)S(1)} %iota_compare_fusion), kind=kOutput, calls=%fused_computation.29 | convolution fusion | flops 405798912 | bytes 6815792 | tf_op jit(solution)/shard_map/kpui,kir->kpur/dot_general | solution.py:58
  171.3 4.9 %fusion.25 = f32[4,128,128]{2,0,1:T(4,128)S(1)} fusion(f32[16,3,128,128]{3,2,1,0:T(8,128)} %fusion.16, s32[16,3]{0,1:T(4,128)S(1)} %copy.93), kind=kOutput, calls=%fused_computation.39 | convolution fusion | flops 37748928 | bytes 3408064 | tf_op jit(solution)/shard_map/kpb,kpur->bur/dot_general | solution.py:61
  176.1 2.9 fusion.22
  179.1 0.1 copy.99
  179.2 0.1 copy.100
  179.4 145.6 %all-reduce.2.cloned.1.call-done = f32[128,128]{1,0:T(8,128)} async-done(((f32[128,128]{1,0:T(8,128)}), f32[128,128]{1,0:T(8,128)}) %all-reduce.2.cloned.1.call-update) | async-done | bytes 65552 | tf_op jit(solution)/shard_map/psum | solution.py:96
  324.9 1.2 fusion.49
  326.1 0.1 copy.118
  326.3 1.9 gather_fusion.5
  328.2 4.3 %fusion.15 = f32[16,3,128,128]{3,2,1,0:T(8,128)} fusion(bf16[16,128,128,1]{2,1,3,0:T(8,128)(2,1)S(1)} %bitcast.101, bf16[16,3,128,128]{3,2,1,0:T(8,128)(2,1)} %bitcast.111, bf16[16,3,128,128]{3,2,1,0:T(8,128)(2,1)S(1)} %bitcast.105, pred[16,3]{1,0:T(8,128)(4,1)S(1)} %iota_compare_fusion), kind=kOutput, calls=%fused_computation.28 | convolution fusion | flops 405798912 | bytes 6815792 | tf_op jit(solution)/shard_map/kpui,kir->kpur/dot_general | solution.py:58
  332.5 3.6 copy.113
  336.1 3.1 fusion.44
  339.2 0.5 multiply_reduce_fusion.2
  339.9 0.1 copy.121
  340.0 1.9 gather_fusion.6
  341.9 4.1 %fusion.14 = f32[16,3,128,128]{3,2,1,0:T(8,128)} fusion(bf16[16,128,128,1]{2,1,3,0:T(8,128)(2,1)S(1)} %bitcast.102, bf16[16,3,128,128]{3,2,1,0:T(8,128)(2,1)} %bitcast.110, bf16[16,3,128,128]{3,2,1,0:T(8,128)(2,1)S(1)} %bitcast.106, pred[16,3]{1,0:T(8,128)(4,1)S(1)} %iota_compare_fusion), kind=kOutput, calls=%fused_computation.27 | convolution fusion | flops 405798912 | bytes 6815792 | tf_op jit(solution)/shard_map/kpui,kir->kpur/dot_general | solution.py:58
  346.0 3.6 copy.116
  349.6 3.1 fusion.42
  352.7 0.5 multiply_reduce_fusion
  353.2 0.1 multiply_subtract_fusion
  353.3 0.8 copy.109
  354.1 0.8 copy.108
  (44 shorter events, 1.4 us)
Async XLA Ops:
  7.2 150.4 %copy-start = (s32[1,192]{1,0:T(1,128)S(1)}, s32[1,192]{1,0:T(1,128)}, u32[]{:S(2)}) copy-start(s32[1,192]{1,0:T(1,128)} %param.11) | copy-start | bytes 2308
  9.8 24.9 %all-to-all-start = ((s32[48,1,1]{2,1,0:T(1,128)}), s32[48,1,1]{2,1,0:T(1,128)S(1)}, u32[]{:S(2)}, u32[]{:S(2)}) async-start(s32[48,1,1]{2,1,0:T(1,128)} %copy.87), calls=%async_computation | async-start | bytes 49152 | tf_op jit(solution)/shard_map/all_to_all | solution.py:29
  34.8 15.0 %all-to-all-start.1 = ((s32[48,1,1]{2,1,0:T(1,128)}), s32[48,1,1]{2,1,0:T(1,128)S(1)}, u32[]{:S(2)}, u32[]{:S(2)}) async-start(s32[48,1,1]{2,1,0:T(1,128)} %copy.91), calls=%async_computation.1 | async-start | bytes 49152 | tf_op jit(solution)/shard_map/all_to_all | solution.py:30
  43.5 12.6 %copy-start.4 = (bf16[128,128]{1,0:T(8,128)(2,1)S(1)}, bf16[128,128]{1,0:T(8,128)(2,1)}, u32[]{:S(2)}) copy-start(bf16[128,128]{1,0:T(8,128)(2,1)} %param.7) | copy-start | bytes 98308
  43.5 13.5 %copy-start.1 = (bf16[512,128]{1,0:T(8,128)(2,1)S(1)}, bf16[512,128]{1,0:T(8,128)(2,1)}, u32[]{:S(2)}) copy-start(bf16[512,128]{1,0:T(8,128)(2,1)} %param.6) | copy-start | bytes 393220
  49.8 112.7 %all-to-all-start.2 = ((bf16[48,128,128]{2,1,0:T(8,128)(2,1)}), bf16[48,128,128]{2,1,0:T(8,128)(2,1)}, u32[]{:S(2)}, u32[]{:S(2)}) async-start(bf16[48,128,128]{2,1,0:T(8,128)(2,1)} %fusion.11), calls=%async_computation.2 | async-start | bytes 3145728 | tf_op jit(solution)/shard_map/all_to_all | solution.py:28
  56.1 268.8 %all-reduce.2.cloned.1.call-start = ((), (), s32[]{:S(2)}) async-start(), calls=%async_computation.3 | async-start | bytes 131072 | tf_op jit(solution)/shard_map/psum | solution.py:96
  171.3 4.9 %copy-start.2 = (f32[16,3,128,128]{3,2,1,0:T(8,128)S(1)}, f32[16,3,128,128]{3,2,1,0:T(8,128)}, u32[]{:S(2)}) copy-start(f32[16,3,128,128]{3,2,1,0:T(8,128)} %fusion.9) | copy-start | bytes 9437188
  336.1 3.1 copy-start.3
Sparse Core Ops, SparseCore 0:
  60.7 264.1 all-reduce.1
where the time goes:
time: 362 us
  waiting for transfers between devices  160 us (44%)
  blocking collectives  95.8 us (26%)
  matrix products  31.7 us (9%)
  starting transfers between devices  27.3 us (8%)
  local copies, waits for them, and re-layouts  24 us (7%)
  between operations  14.3 us (4%)
  other arithmetic  8.24 us (2%)
    psum x1, waiting for transfers between devices, body(): gram_matrix = lax.psum(local_gram, 'blk')  146 us
    all_gather x1, blocking collectives, visit_panels(): lax.all_gather(item_factors, 'blk', axis=0, tiled=True)  95.8 us
    all_to_all x1, starting transfers between devices, body(): lax.all_to_all(picked_rows, 'dev', split_axis=0, concat_axis=0, tiled=True)  15.5 us
    dot_general x3, matrix products, block_products(): jnp.einsum('kpui,kir->kpur', scaled, item_rows, preferred_element_type=jn...  12.5 us
    dot_general x3, matrix products, block_products(): jnp.einsum('kpb,kpur->bur', scatter_table, carried, precision=lax.Precisi...  11 us
    all_to_all x1, waiting for transfers between devices, body(): lax.all_to_all(picked_rows, 'dev', split_axis=0, concat_axis=0, tiled=True)  8.58 us
  transfers between devices with their start and end apart: 4, of which 3 were waited for; matrix products, arithmetic and copies ran while one was open for 9% of the time, Pallas kernels for 0%

commit v1 on v0

v1 whole, which is shorter than its diff:
```python
import jax
import jax.numpy as jnp
from jax import lax
from jax.experimental import pallas as pl
from jax.experimental.pallas import tpu as pltpu
from jax.sharding import PartitionSpec as P

ITERS = 2

ridge_weight = 0.5
epsilon = 1e-06


META_ROWS = 8


def pick_kernel(cols_ref, rows_ref, place_ref, values_ref, out_ref, staged, read_sem, write_sem):
    holders, _, width = out_ref.shape
    edge = values_ref.shape[1]
    user_blocks = place_ref.shape[1] // holders
    panels = lax.axis_size("blk")
    for holder in range(holders):
        second = (cols_ref[2 * holder + 1] >= 0).astype(jnp.int32)
        pltpu.make_async_copy(
            values_ref.at[2 * holder + second], staged.at[holder, pl.ds(0, edge)], read_sem
        ).start()
    for holder in range(holders):
        col = jnp.maximum(cols_ref[2 * holder], cols_ref[2 * holder + 1])
        second = (cols_ref[2 * holder + 1] >= 0).astype(jnp.int32)
        place = place_ref[0, rows_ref[2 * holder + second]] % user_blocks
        code = jnp.where(col >= 0, place * panels + col, -1)
        staged[holder, edge:, :] = jnp.full((META_ROWS, width), code.astype(jnp.float32)).astype(staged.dtype)
    pltpu.make_async_copy(values_ref.at[pl.ds(0, holders)], staged.at[:, pl.ds(0, edge)], read_sem).wait()
    write = pltpu.make_async_copy(staged, out_ref, write_sem)
    write.start()
    write.wait()


def pick_blocks(block_cols, block_rows, row_place, block_values):
    slots, edge, width = block_values.shape
    out = (slots // 2, edge + META_ROWS, width)
    smem = pl.BlockSpec(memory_space=pltpu.SMEM)
    return pl.pallas_call(
        pick_kernel,
        out_shape=jax.ShapeDtypeStruct(out, block_values.dtype),
        in_specs=[smem, smem, smem, pl.BlockSpec(memory_space=pl.ANY)],
        out_specs=pl.BlockSpec(memory_space=pl.ANY),
        scratch_shapes=[
            pltpu.VMEM(out, block_values.dtype),
            pltpu.SemaphoreType.DMA,
            pltpu.SemaphoreType.DMA,
        ],
    )(block_cols, block_rows, row_place, block_values)


def cg_kernel(
    blocks_ref, items_ref, gram_ref, factors_ref, solution_ref, residual_ref,
    weights, meta, codes_vmem, codes_ref, meta_sem, code_sem, sems,
):
    slots = blocks_ref.shape[0]
    edge = blocks_ref.shape[1] - META_ROWS
    items = items_ref.shape[0]
    panels = items // edge
    chunk = 2 * edge

    meta_copy = pltpu.make_async_copy(blocks_ref.at[:, pl.ds(edge, META_ROWS)], meta, meta_sem)
    meta_copy.start()
    weights[...] = jnp.zeros_like(weights)
    meta_copy.wait()
    codes_vmem[...] = jnp.max(meta[...].astype(jnp.float32), axis=1).astype(jnp.int32)
    code_copy = pltpu.make_async_copy(codes_vmem, codes_ref, code_sem)
    code_copy.start()
    code_copy.wait()

    def block_copy(slot):
        code = codes_ref[slot, 0]
        user = pl.multiple_of((code // panels) * edge, edge)
        item = pl.multiple_of((code % panels) * edge, edge)
        return pltpu.make_async_copy(
            blocks_ref.at[slot, pl.ds(0, edge)], weights.at[pl.ds(user, edge), pl.ds(item, edge)], sems.at[slot]
        )

    for slot in range(slots):
        pl.when(codes_ref[slot, 0] >= 0)(lambda slot=slot: block_copy(slot).start())

    def rest(vector):
        return (
            jnp.dot(vector, gram_ref[...], precision=lax.Precision.HIGHEST, preferred_element_type=jnp.float32)
            + ridge_weight * vector
        )

    solution = factors_ref[...].astype(jnp.float32)
    first_rest = rest(solution)

    for slot in range(slots):
        pl.when(codes_ref[slot, 0] >= 0)(lambda slot=slot: block_copy(slot).wait())

    def products(direction, with_rhs):
        total = rhs = None
        for start in range(0, items, chunk):
            rows = items_ref[start : start + chunk, :]
            held = weights[:, start : start + chunk].astype(jnp.float32)
            scores = lax.dot_general(
                direction, rows, (((1,), (1,)), ((), ())), preferred_element_type=jnp.float32
            )
            scaled = (scores * held).astype(jnp.bfloat16)
            part = jnp.dot(scaled, rows, preferred_element_type=jnp.float32)
            total = part if total is None else total + part
            if with_rhs:
                confidence = jnp.where(held > 0, 1.0 + held, 0.0).astype(jnp.bfloat16)
                lifted = jnp.dot(confidence, rows, preferred_element_type=jnp.float32)
                rhs = lifted if rhs is None else rhs + lifted
        return total, rhs

    block_sum, rhs = products(factors_ref[...], True)
    residual = rhs - (block_sum + first_rest)
    direction = residual
    norm_now = jnp.sum(residual * residual, axis=1, keepdims=True)
    for sweep in range(ITERS):
        block_sum, _ = products(direction.astype(jnp.bfloat16), False)
        image = block_sum + rest(direction)
        curvature = jnp.sum(direction * image, axis=1, keepdims=True)
        step_length = norm_now / (curvature + epsilon)
        solution = solution + step_length * direction
        residual = residual - step_length * image
        if sweep + 1 < ITERS:
            norm_next = jnp.sum(residual * residual, axis=1, keepdims=True)
            direction = residual + (norm_next / (norm_now + epsilon)) * direction
            norm_now = norm_next
    solution_ref[...] = solution
    residual_ref[...] = residual


def run_cg(blocks, items, gram, factors):
    users, rank = factors.shape
    slots = blocks.shape[0]
    out = jax.ShapeDtypeStruct((users, rank), jnp.float32)
    vmem = pl.BlockSpec(memory_space=pltpu.VMEM)
    return pl.pallas_call(
        cg_kernel,
        out_shape=(out, out),
        in_specs=[pl.BlockSpec(memory_space=pl.ANY), vmem, vmem, vmem],
        out_specs=(vmem, vmem),
        scratch_shapes=[
            pltpu.VMEM((users, items.shape[0]), blocks.dtype),
            pltpu.VMEM((slots, META_ROWS, rank), blocks.dtype),
            pltpu.VMEM((slots, rank), jnp.int32),
            pltpu.SMEM((slots, rank), jnp.int32),
            pltpu.SemaphoreType.DMA,
            pltpu.SemaphoreType.DMA,
            pltpu.SemaphoreType.DMA((slots,)),
        ],
        compiler_params=pltpu.CompilerParams(vmem_limit_bytes=40 << 20),
    )(blocks, items, gram, factors)


def body(factors, item_factors, block_values, block_rows, block_cols, row_place):
    group_count = lax.axis_size("blk")
    half = lax.axis_index("blk") % 2

    other = lax.ppermute(item_factors, "blk", [(i, i ^ 1) for i in range(group_count)])
    picked = pick_blocks(block_cols, block_rows, row_place, block_values)
    picked, other = lax.optimization_barrier((picked, other))
    blocks = lax.all_to_all(picked, "dev", split_axis=0, concat_axis=0, tiled=True)
    pair = jnp.concatenate(
        [jnp.where(half == 0, item_factors, other), jnp.where(half == 0, other, item_factors)]
    )
    halves = [[2 * i + h for i in range(group_count // 2)] for h in range(2)]
    items = lax.all_gather(pair, "blk", axis=0, tiled=True, axis_index_groups=halves)
    gram = jnp.dot(items.T, items, preferred_element_type=jnp.float32)
    return run_cg(blocks, items, gram, factors)


def solution(mesh):
    return jax.shard_map(
        body,
        mesh=mesh,
        in_specs=(
            P(("blk", "dev"), None),
            P("blk", None),
            P(("blk", "dev"), None, None),
            P(("blk", "dev")),
            P(("blk", "dev")),
            P("blk", None),
        ),
        out_specs=(P(("blk", "dev"), None), P(("blk", "dev"), None)),
        check_vma=False,
    )
```

time: 362 us -> 99.1 us (0.27)
  the two profiles are of different devices: /device:TPU:2 before, /device:TPU:1 now
where the time goes in v1:
time: 99.1 us; the launch traced here: 98.7 us
  waiting for transfers between devices  37.1 us (37%)
  starting transfers between devices  25.9 us (26%)
  blocking collectives  22.5 us (23%)
  Pallas kernels  12.2 us (12%)
    all_to_all x1, waiting for transfers between devices, body(): lax.all_to_all(picked, 'dev', split_axis=0, concat_axis=0, tiled=True)  37.1 us
    all_gather x1, blocking collectives, body(): lax.all_gather(pair, 'blk', axis=0, tiled=True, axis_index_groups=halves)  22.5 us
    ppermute x1, starting transfers between devices, body(): lax.ppermute(item_factors, 'blk', [(i, i ^ 1) for i in range(group_count)])  15.7 us
    all_to_all x1, starting transfers between devices, body(): lax.all_to_all(picked, 'dev', split_axis=0, concat_axis=0, tiled=True)  10.2 us
    pallas_call x1, Pallas kernels, run_cg(): pl.pallas_call(cg_kernel, out_shape=(out, out), in_specs=[pl.BlockSpec(me...  8.92 us
    pallas_call x1, Pallas kernels, pick_blocks(): pl.pallas_call(pick_kernel, out_shape=jax.ShapeDtypeStruct(out, block_val...  3.24 us
  transfers between devices with their start and end apart: 2, of which 1 were waited for; matrix products, arithmetic and copies ran while one was open for 0% of the time, Pallas kernels for 3%

profile of v1, /device:TPU:1, one launch (start us, length us, event | category | flops | bytes accessed | tf_op | source)
XLA Modules:
  0.0 98.7 jit_solution(12830473593716449060)
XLA Ops:
  0.6 15.7 %collective-permute-start = (bf16[128,128]{1,0:T(8,128)(2,1)}, bf16[128,128]{1,0:T(8,128)(2,1)S(1)}, u32[]{:S(2)}, u32[]{:S(2)}) collective-permute-start(bf16[128,128]{1,0:T(8,128)(2,1)} %param.7), channel_id=1, source_target_pairs={{0,48},{48,0},{96,144},{144,96},{192,240},{240,192},{288,336},{336... | collective-permute-start | bytes 98312 | tf_op jit(solution)/shard_map/ppermute | solution.py:161
  16.3 3.2 %shard_map.77 = bf16[48,136,128]{2,1,0:T(8,128)(2,1)} custom-call(s32[96]{0:T(128)} %cols_ref.1, s32[96]{0:T(128)} %rows_ref.1, s32[1,192]{1,0:T(1,128)} %place_ref.1, bf16[96,128,128]{2,1,0:T(8,128)(2,1)} %values_ref.1), custom_call_target="tpu_custom_call" | custom-call | tf_op jit(solution)/shard_map/pallas_call | solution.py:43
  19.6 0.0 copy-start.1
  19.6 0.0 collective-permute-done
  19.6 10.2 %all-to-all-start = ((bf16[48,136,128]{2,1,0:T(8,128)(2,1)}), bf16[48,136,128]{2,1,0:T(8,128)(2,1)S(1)}, u32[]{:S(2)}, u32[]{:S(2)}) async-start(bf16[48,136,128]{2,1,0:T(8,128)(2,1)} %shard_map.77), calls=%async_computation | async-start | bytes 3342336 | tf_op jit(solution)/shard_map/all_to_all | solution.py:164
  29.8 0.0 copy-start
  29.8 0.0 copy-done.1
  29.9 22.5 %all_gather.3.items_ref = bf16[2048,128]{1,0:T(8,128)(2,1)S(1)} all-gather(bf16[256,128]{1,0:T(8,128)(2,1)S(1)} %pad_maximum_fusion), channel_id=1, replica_groups={{0,96,192,288,384,480,576,672},{48,144,240,336,432,528,624,720},{1,97,1..., dimensions={0}, use_global_device_ids=true | all-gather | bytes 589824 | tf_op jit(solution)/shard_map/all_gather | solution.py:169
  52.3 0.3 fusion.gram_ref
  52.7 37.1 %all-to-all-done.blocks_ref = bf16[48,136,128]{2,1,0:T(8,128)(2,1)S(1)} async-done(((bf16[48,136,128]{2,1,0:T(8,128)(2,1)}), bf16[48,136,128]{2,1,0:T(8,128)(2,1)S(1)}, u32[]{:S(2)}, u32[]{:S(2)}) %all-to-all-start) | async-done | bytes 1671200 | tf_op jit(solution)/shard_map/all_to_all | solution.py:164
  89.8 0.0 copy-done
  89.8 8.9 %shard_map.78 = (f32[512,128]{1,0:T(8,128)}, f32[512,128]{1,0:T(8,128)}) custom-call(bf16[48,136,128]{2,1,0:T(8,128)(2,1)S(1)} %all-to-all-done.blocks_ref, bf16[2048,128]{1,0:T(8,128)(2,1)S(1)} %all_gather.3.items_ref, f32[128,128]{1,0:T(8,128)S(1)} %fusion.gram_ref, bf16[512,128]{1,0:T(8,128)(2,1)S(1)} %copy-done), custom_call_target="tpu_custom_call" | custom-call | tf_op jit(solution)/shard_map/pallas_call | solution.py:139
  (2 shorter events, 0.0 us)
Async XLA Ops:
  0.6 19.0 %collective-permute-start = (bf16[128,128]{1,0:T(8,128)(2,1)}, bf16[128,128]{1,0:T(8,128)(2,1)S(1)}, u32[]{:S(2)}, u32[]{:S(2)}) collective-permute-start(bf16[128,128]{1,0:T(8,128)(2,1)} %param.7), channel_id=1, source_target_pairs={{0,48},{48,0},{96,144},{144,96},{192,240},{240,192},{288,336},{336... | collective-permute-start | bytes 98312 | tf_op jit(solution)/shard_map/ppermute | solution.py:161
  19.6 10.2 %copy-start.1 = (bf16[128,128]{1,0:T(8,128)(2,1)S(1)}, bf16[128,128]{1,0:T(8,128)(2,1)}, u32[]{:S(2)}) copy-start(bf16[128,128]{1,0:T(8,128)(2,1)} %param.7) | copy-start | bytes 98308
  19.6 70.2 %all-to-all-start = ((bf16[48,136,128]{2,1,0:T(8,128)(2,1)}), bf16[48,136,128]{2,1,0:T(8,128)(2,1)S(1)}, u32[]{:S(2)}, u32[]{:S(2)}) async-start(bf16[48,136,128]{2,1,0:T(8,128)(2,1)} %shard_map.77), calls=%async_computation | async-start | bytes 3342336 | tf_op jit(solution)/shard_map/all_to_all | solution.py:164
  29.8 60.0 %copy-start = (bf16[512,128]{1,0:T(8,128)(2,1)S(1)}, bf16[512,128]{1,0:T(8,128)(2,1)}, u32[]{:S(2)}) copy-start(bf16[512,128]{1,0:T(8,128)(2,1)} %factors_ref.1) | copy-start | bytes 393220

commit v2 on v1

v2 whole, which is shorter than its diff:
```python
import jax
import jax.numpy as jnp
from jax import lax
from jax.experimental import pallas as pl
from jax.experimental.pallas import tpu as pltpu
from jax.sharding import PartitionSpec as P

ITERS = 2

ridge_weight = 0.5
epsilon = 1e-06


CHIPS_X, CORES = 4, 2
CHUNK = 512
META_ROWS = 8


def pick_kernel(cols_ref, rows_ref, place_ref, values_ref, out_ref, staged, read_sems, write_sem):
    holders, _, width = out_ref.shape
    edge = values_ref.shape[1]
    user_blocks = place_ref.shape[1] // holders
    panels = lax.axis_size("blk")
    parts = read_sems.shape[0]
    share = holders // parts
    for holder in range(holders):
        second = (cols_ref[2 * holder + 1] >= 0).astype(jnp.int32)
        pltpu.make_async_copy(
            values_ref.at[2 * holder + second],
            staged.at[holder, pl.ds(0, edge)],
            read_sems.at[holder // share],
        ).start()
    for part in range(parts):
        own = pl.ds(part * share, share)
        for holder in range(part * share, (part + 1) * share):
            col = jnp.maximum(cols_ref[2 * holder], cols_ref[2 * holder + 1])
            second = (cols_ref[2 * holder + 1] >= 0).astype(jnp.int32)
            place = place_ref[0, rows_ref[2 * holder + second]] % user_blocks
            code = jnp.where(col >= 0, place * panels + col, -1)
            staged[holder, edge:, :] = jnp.full((META_ROWS, width), code.astype(jnp.float32)).astype(staged.dtype)
        pltpu.make_async_copy(values_ref.at[own], staged.at[own, pl.ds(0, edge)], read_sems.at[part]).wait()
        pltpu.make_async_copy(staged.at[own], out_ref.at[own], write_sem).start()
    pltpu.make_async_copy(staged, out_ref, write_sem).wait()


def pick_blocks(block_cols, block_rows, row_place, block_values):
    slots, edge, width = block_values.shape
    out = (slots // 2, edge + META_ROWS, width)
    smem = pl.BlockSpec(memory_space=pltpu.SMEM)
    return pl.pallas_call(
        pick_kernel,
        out_shape=jax.ShapeDtypeStruct(out, block_values.dtype),
        in_specs=[smem, smem, smem, pl.BlockSpec(memory_space=pl.ANY)],
        out_specs=pl.BlockSpec(memory_space=pl.ANY),
        scratch_shapes=[
            pltpu.VMEM(out, block_values.dtype),
            pltpu.SemaphoreType.DMA((4,)),
            pltpu.SemaphoreType.DMA,
        ],
    )(block_cols, block_rows, row_place, block_values)


def dense_part(vector, gram):
    product = jnp.dot(vector, gram, precision=lax.Precision.HIGHEST, preferred_element_type=jnp.float32)
    return product + ridge_weight * vector


def cg_kernel(
    blocks_ref, items, turned, gram, rest, factors, solution_ref, residual_ref,
    weights, first_scores, meta, codes_vmem, codes, meta_sem, code_sem, block_sems,
):
    slots = blocks_ref.shape[0]
    edge = blocks_ref.shape[1] - META_ROWS
    count = items.shape[0]
    panels = count // edge

    meta_copy = pltpu.make_async_copy(blocks_ref.at[:, pl.ds(edge, META_ROWS)], meta, meta_sem)
    meta_copy.start()
    weights[...] = jnp.zeros_like(weights)
    meta_copy.wait()
    codes_vmem[...] = jnp.max(meta[...].astype(jnp.float32), axis=1).astype(jnp.int32)
    code_copy = pltpu.make_async_copy(codes_vmem, codes, code_sem)
    code_copy.start()
    code_copy.wait()

    def block_copy(slot):
        code = codes[slot, 0]
        user = pl.multiple_of((code // panels) * edge, edge)
        item = pl.multiple_of((code % panels) * edge, edge)
        return pltpu.make_async_copy(
            blocks_ref.at[slot, pl.ds(0, edge)],
            weights.at[pl.ds(user, edge), pl.ds(item, edge)],
            block_sems.at[slot],
        )

    for slot in range(slots):
        pl.when(codes[slot, 0] >= 0)(lambda slot=slot: block_copy(slot).start())

    chunks = [slice(start, start + CHUNK) for start in range(0, count, CHUNK)]

    def scores_of(direction, chunk):
        return jnp.dot(direction, turned[:, chunk], preferred_element_type=jnp.float32)

    for chunk in chunks:
        first_scores[:, chunk] = scores_of(factors[...], chunk)
    for slot in range(slots):
        pl.when(codes[slot, 0] >= 0)(lambda slot=slot: block_copy(slot).wait())

    block_sum = jnp.zeros(factors.shape, jnp.float32)
    rhs = jnp.zeros(factors.shape, jnp.float32)
    for chunk in chunks:
        held = weights[:, chunk].astype(jnp.float32)
        scaled = (first_scores[:, chunk] * held).astype(jnp.bfloat16)
        block_sum += jnp.dot(scaled, items[chunk, :], preferred_element_type=jnp.float32)
        confidence = jnp.where(held > 0, 1.0 + held, 0.0).astype(jnp.bfloat16)
        rhs += jnp.dot(confidence, items[chunk, :], preferred_element_type=jnp.float32)

    solution = factors[...].astype(jnp.float32)
    residual = rhs - (block_sum + rest[...])
    direction = residual
    norm_now = jnp.sum(residual * residual, axis=1, keepdims=True)
    for sweep in range(ITERS):
        rounded = direction.astype(jnp.bfloat16)
        image = dense_part(direction, gram[...])
        for chunk in chunks:
            scaled = (scores_of(rounded, chunk) * weights[:, chunk].astype(jnp.float32)).astype(jnp.bfloat16)
            image += jnp.dot(scaled, items[chunk, :], preferred_element_type=jnp.float32)
        curvature = jnp.sum(direction * image, axis=1, keepdims=True)
        step_length = norm_now / (curvature + epsilon)
        solution = solution + step_length * direction
        residual = residual - step_length * image
        if sweep + 1 < ITERS:
            norm_next = jnp.sum(residual * residual, axis=1, keepdims=True)
            direction = residual + (norm_next / (norm_now + epsilon)) * direction
            norm_now = norm_next
    solution_ref[...] = solution
    residual_ref[...] = residual


def run_cg(blocks, items, turned, gram, first_rest, factors):
    users, rank = factors.shape
    count, slots = items.shape[0], blocks.shape[0]
    out = jax.ShapeDtypeStruct((users, rank), jnp.float32)
    vmem = pl.BlockSpec(memory_space=pltpu.VMEM)
    return pl.pallas_call(
        cg_kernel,
        out_shape=(out, out),
        in_specs=[pl.BlockSpec(memory_space=pl.ANY)] + [vmem] * 5,
        out_specs=(vmem, vmem),
        scratch_shapes=[
            pltpu.VMEM((users, count), blocks.dtype),
            pltpu.VMEM((users, count), jnp.float32),
            pltpu.VMEM((slots, META_ROWS, rank), blocks.dtype),
            pltpu.VMEM((slots, rank), jnp.int32),
            pltpu.SMEM((slots, rank), jnp.int32),
            pltpu.SemaphoreType.DMA,
            pltpu.SemaphoreType.DMA,
            pltpu.SemaphoreType.DMA((slots,)),
        ],
        compiler_params=pltpu.CompilerParams(vmem_limit_bytes=40 << 20),
    )(blocks, items, turned, gram, first_rest, factors)


def border_pairs(group_count, dev_count, depth):
    runs = dev_count // (CHIPS_X * CORES)
    pairs = []
    for group in range(group_count):
        for column in range(CHIPS_X * CORES):
            x, core = divmod(column, CORES)
            for source, target in ((0, runs - 1 - depth), (runs - 1, depth)):
                pairs.append(
                    (
                        group * dev_count + (x * runs + source) * CORES + core,
                        (group ^ 1) * dev_count + (x * runs + target) * CORES + core,
                    )
                )
    return pairs


def from_other_group(block):
    group_count, dev_count = lax.axis_size("blk"), lax.axis_size("dev")
    runs = dev_count // (CHIPS_X * CORES)
    place = (lax.axis_index("dev") // CORES) % runs
    depth = jnp.minimum(place, runs - 1 - place)
    result = None
    for behind in reversed(range(runs // 2)):
        got = lax.ppermute(block, ("blk", "dev"), border_pairs(group_count, dev_count, behind))
        result = got if result is None else jnp.where(depth == behind, got, result)
    return result


def body(factors, item_factors, block_values, block_rows, block_cols, row_place):
    group_count = lax.axis_size("blk")
    half = lax.axis_index("blk") % 2

    other = from_other_group(item_factors)
    picked = pick_blocks(block_cols, block_rows, row_place, block_values)
    blocks = lax.all_to_all(picked, "dev", split_axis=0, concat_axis=0, tiled=True)
    pair = jnp.concatenate(
        [jnp.where(half == 0, item_factors, other), jnp.where(half == 0, other, item_factors)]
    )
    halves = [[2 * i + h for i in range(group_count // 2)] for h in range(2)]
    items = lax.all_gather(pair, "blk", axis=0, tiled=True, axis_index_groups=halves)
    turned = items.T
    gram = jnp.dot(turned, items, preferred_element_type=jnp.float32)
    first_rest = dense_part(factors.astype(jnp.float32), gram)
    return run_cg(blocks, items, turned, gram, first_rest, factors)


def solution(mesh):
    return jax.shard_map(
        body,
        mesh=mesh,
        in_specs=(
            P(("blk", "dev"), None),
            P("blk", None),
            P(("blk", "dev"), None, None),
            P(("blk", "dev")),
            P(("blk", "dev")),
            P("blk", None),
        ),
        out_specs=(P(("blk", "dev"), None), P(("blk", "dev"), None)),
        check_vma=False,
    )
```

time: 99.1 us -> 89.9 us (0.907)
  waiting for transfers between devices: 37.1 us -> 23.4 us
  starting transfers between devices: 25.9 us -> 29 us
    all_to_all x1, waiting for transfers between devices: 37.1 us -> 22.5 us  [body(): lax.all_to_all(picked, 'dev', split_axis=0, concat_axis=0, tiled=True)]
    all_to_all x1, starting transfers between devices: 10.2 us -> 16.4 us  [body(): lax.all_to_all(picked, 'dev', split_axis=0, concat_axis=0, tiled=True)]
    ppermute x1 -> x3, starting transfers between devices: 15.7 us -> 12.5 us  [from_other_group(): lax.ppermute(block, ('blk', 'dev'), border_pairs(group_count, dev_count,...]
  transfers between devices with their start and end apart: 2 -> 4, of which waited for: 1 -> 2; matrix products, arithmetic and copies ran while one was open for 0% -> 1% of each run, Pallas kernels for 3% -> 0%
where the time goes in v2:
time: 89.9 us; the launch traced here: 89.5 us
  starting transfers between devices  29 us (32%)
  waiting for transfers between devices  23.4 us (26%)
  blocking collectives  22.8 us (25%)
  Pallas kernels  12.4 us (14%)
    all_gather x1, blocking collectives, body(): lax.all_gather(pair, 'blk', axis=0, tiled=True, axis_index_groups=halves)  22.8 us
    all_to_all x1, waiting for transfers between devices, body(): lax.all_to_all(picked, 'dev', split_axis=0, concat_axis=0, tiled=True)  22.5 us
    all_to_all x1, starting transfers between devices, body(): lax.all_to_all(picked, 'dev', split_axis=0, concat_axis=0, tiled=True)  16.4 us
    ppermute x3, starting transfers between devices, from_other_group(): lax.ppermute(block, ('blk', 'dev'), border_pairs(group_count, dev_count,...  12.5 us
    pallas_call x1, Pallas kernels, run_cg(): pl.pallas_call(cg_kernel, out_shape=(out, out), in_specs=[pl.BlockSpec(me...  9.5 us
    pallas_call x1, Pallas kernels, pick_blocks(): pl.pallas_call(pick_kernel, out_shape=jax.ShapeDtypeStruct(out, block_val...  2.9 us
  transfers between devices with their start and end apart: 4, of which 2 were waited for; matrix products, arithmetic and copies ran while one was open for 1% of the time, Pallas kernels for 0%

profile of v2, /device:TPU:1, one launch (start us, length us, event | category | flops | bytes accessed | tf_op | source)
XLA Modules:
  0.0 89.5 jit_solution(10402038014496975350)
XLA Ops:
  0.6 2.9 %shard_map.77 = bf16[48,136,128]{2,1,0:T(8,128)(2,1)} custom-call(s32[96]{0:T(128)} %cols_ref.1, s32[96]{0:T(128)} %rows_ref.1, s32[1,192]{1,0:T(1,128)} %place_ref.1, bf16[96,128,128]{2,1,0:T(8,128)(2,1)} %values_ref.1), custom_call_target="tpu_custom_call" | custom-call | tf_op jit(solution)/shard_map/pallas_call | solution.py:50
  3.5 0.0 copy-start.1
  3.6 16.4 %all-to-all-start = ((bf16[48,136,128]{2,1,0:T(8,128)(2,1)}), bf16[48,136,128]{2,1,0:T(8,128)(2,1)S(1)}, u32[]{:S(2)}, u32[]{:S(2)}) async-start(bf16[48,136,128]{2,1,0:T(8,128)(2,1)} %shard_map.77), calls=%async_computation | async-start | bytes 3342336 | tf_op jit(solution)/shard_map/all_to_all | solution.py:198
  20.0 0.0 copy-done.1
  20.0 0.0 copy-start
  20.0 0.1 copy.11
  20.1 10.0 %collective-permute-start = (bf16[128,128]{0,1:T(8,128)(2,1)S(1)}, bf16[128,128]{0,1:T(8,128)(2,1)S(1)}, u32[]{:S(2)}, u32[]{:S(2)}) collective-permute-start(bf16[128,128]{0,1:T(8,128)(2,1)S(1)} %copy.11), channel_id=1, source_target_pairs={{0,58},{10,48},{1,59},{11,49},{12,70},{22,60},{13,71},{23,61},{24,... | collective-permute-start | bytes 98312 | tf_op jit(solution)/shard_map/ppermute | solution.py:187
  30.1 1.3 %collective-permute-start.1 = (bf16[128,128]{0,1:T(8,128)(2,1)S(1)}, bf16[128,128]{0,1:T(8,128)(2,1)S(1)}, u32[]{:S(2)}, u32[]{:S(2)}) collective-permute-start(bf16[128,128]{0,1:T(8,128)(2,1)S(1)} %copy.11), channel_id=1, source_target_pairs={{0,56},{10,50},{1,57},{11,51},{12,68},{22,62},{13,69},{23,63},{24,... | collective-permute-start | bytes 98312 | tf_op jit(solution)/shard_map/ppermute | solution.py:187
  31.4 1.3 %collective-permute-start.2 = (bf16[128,128]{0,1:T(8,128)(2,1)S(1)}, bf16[128,128]{0,1:T(8,128)(2,1)S(1)}, u32[]{:S(2)}, u32[]{:S(2)}) collective-permute-start(bf16[128,128]{0,1:T(8,128)(2,1)S(1)} %copy.11), channel_id=1, source_target_pairs={{0,54},{10,52},{1,55},{11,53},{12,66},{22,64},{13,67},{23,65},{24,... | collective-permute-start | bytes 98312 | tf_op jit(solution)/shard_map/ppermute | solution.py:187
  32.8 0.0 collective-permute-done
  32.8 0.0 collective-permute-done.1
  32.8 0.9 %collective-permute-done.2 = bf16[128,128]{0,1:T(8,128)(2,1)S(1)} collective-permute-done((bf16[128,128]{0,1:T(8,128)(2,1)S(1)}, bf16[128,128]{0,1:T(8,128)(2,1)S(1)}, u32[]{:S(2)}, u32[]{:S(2)}) %collective-permute-start.2) | collective-permute-done | bytes 32800 | tf_op jit(solution)/shard_map/ppermute | solution.py:187
  33.8 22.8 %all_gather.3 = bf16[2048,128]{0,1:T(8,128)(2,1)S(1)} all-gather(bf16[256,128]{0,1:T(8,128)(2,1)S(1)} %pad_maximum_fusion), channel_id=1, replica_groups={{0,96,192,288,384,480,576,672},{48,144,240,336,432,528,624,720},{1,97,1..., dimensions={0}, use_global_device_ids=true | all-gather | bytes 589824 | tf_op jit(solution)/shard_map/all_gather | solution.py:203
  56.6 0.3 copy.14.items
  56.9 0.3 fusion.1.gram
  57.2 0.0 copy-done
  57.2 0.3 fusion.rest
  57.5 22.5 %all-to-all-done.blocks_ref = bf16[48,136,128]{2,1,0:T(8,128)(2,1)S(1)} async-done(((bf16[48,136,128]{2,1,0:T(8,128)(2,1)}), bf16[48,136,128]{2,1,0:T(8,128)(2,1)S(1)}, u32[]{:S(2)}, u32[]{:S(2)}) %all-to-all-start) | async-done | bytes 1671200 | tf_op jit(solution)/shard_map/all_to_all | solution.py:198
  80.0 9.5 %shard_map.78 = (f32[512,128]{1,0:T(8,128)}, f32[512,128]{1,0:T(8,128)}) custom-call(bf16[48,136,128]{2,1,0:T(8,128)(2,1)S(1)} %all-to-all-done.blocks_ref, bf16[2048,128]{1,0:T(8,128)(2,1)S(1)} %copy.14.items, bf16[128,2048]{1,0:T(8,128)(2,1)S(1)} %bitcast.9, f32[128,128]{1,0:T(8,128)S(1)} %fusion.1.gram, f32[512,128]{1,0:T(8,128)S(1)} %fusion.rest, ...), custom_call_target="tpu_custom_call" | custom-call | tf_op jit(solution)/shard_map/pallas_call | solution.py:145
  (3 shorter events, 0.0 us)
Async XLA Ops:
  3.5 16.5 %copy-start.1 = (bf16[128,128]{1,0:T(8,128)(2,1)S(1)}, bf16[128,128]{1,0:T(8,128)(2,1)}, u32[]{:S(2)}) copy-start(bf16[128,128]{1,0:T(8,128)(2,1)} %param.7) | copy-start | bytes 98308
  3.6 76.4 %all-to-all-start = ((bf16[48,136,128]{2,1,0:T(8,128)(2,1)}), bf16[48,136,128]{2,1,0:T(8,128)(2,1)S(1)}, u32[]{:S(2)}, u32[]{:S(2)}) async-start(bf16[48,136,128]{2,1,0:T(8,128)(2,1)} %shard_map.77), calls=%async_computation | async-start | bytes 3342336 | tf_op jit(solution)/shard_map/all_to_all | solution.py:198
  20.0 37.2 %copy-start = (bf16[512,128]{1,0:T(8,128)(2,1)S(1)}, bf16[512,128]{1,0:T(8,128)(2,1)}, u32[]{:S(2)}) copy-start(bf16[512,128]{1,0:T(8,128)(2,1)} %factors.1) | copy-start | bytes 393220
  20.1 12.6 %collective-permute-start = (bf16[128,128]{0,1:T(8,128)(2,1)S(1)}, bf16[128,128]{0,1:T(8,128)(2,1)S(1)}, u32[]{:S(2)}, u32[]{:S(2)}) collective-permute-start(bf16[128,128]{0,1:T(8,128)(2,1)S(1)} %copy.11), channel_id=1, source_target_pairs={{0,58},{10,48},{1,59},{11,49},{12,70},{22,60},{13,71},{23,61},{24,... | collective-permute-start | bytes 98312 | tf_op jit(solution)/shard_map/ppermute | solution.py:187
  30.1 2.7 %collective-permute-start.1 = (bf16[128,128]{0,1:T(8,128)(2,1)S(1)}, bf16[128,128]{0,1:T(8,128)(2,1)S(1)}, u32[]{:S(2)}, u32[]{:S(2)}) collective-permute-start(bf16[128,128]{0,1:T(8,128)(2,1)S(1)} %copy.11), channel_id=1, source_target_pairs={{0,56},{10,50},{1,57},{11,51},{12,68},{22,62},{13,69},{23,63},{24,... | collective-permute-start | bytes 98312 | tf_op jit(solution)/shard_map/ppermute | solution.py:187
  31.4 2.3 %collective-permute-start.2 = (bf16[128,128]{0,1:T(8,128)(2,1)S(1)}, bf16[128,128]{0,1:T(8,128)(2,1)S(1)}, u32[]{:S(2)}, u32[]{:S(2)}) collective-permute-start(bf16[128,128]{0,1:T(8,128)(2,1)S(1)} %copy.11), channel_id=1, source_target_pairs={{0,54},{10,52},{1,55},{11,53},{12,66},{22,64},{13,67},{23,65},{24,... | collective-permute-start | bytes 98312 | tf_op jit(solution)/shard_map/ppermute | solution.py:187

commit v3 on v2

--- a/solution.py
+++ b/solution.py
@@ -12,13 +12,14 @@
 
 
 CHIPS_X, CORES = 4, 2
-CHUNK = 512
-META_ROWS = 8
+CHUNK = 1024
+PARTS = 2
+META_ROWS = 2
 
 
 def pick_kernel(cols_ref, rows_ref, place_ref, values_ref, out_ref, staged, read_sems, write_sem):
-    holders, _, width = out_ref.shape
-    edge = values_ref.shape[1]
+    holders, _, _, width = out_ref.shape
+    pairs = values_ref.shape[1]
     user_blocks = place_ref.shape[1] // holders
     panels = lax.axis_size("blk")
     parts = read_sems.shape[0]
@@ -27,7 +28,7 @@
         second = (cols_ref[2 * holder + 1] >= 0).astype(jnp.int32)
         pltpu.make_async_copy(
             values_ref.at[2 * holder + second],
-            staged.at[holder, pl.ds(0, edge)],
+            staged.at[holder, pl.ds(0, pairs)],
             read_sems.at[holder // share],
         ).start()
     for part in range(parts):
@@ -37,15 +38,16 @@
             second = (cols_ref[2 * holder + 1] >= 0).astype(jnp.int32)
             place = place_ref[0, rows_ref[2 * holder + second]] % user_blocks
             code = jnp.where(col >= 0, place * panels + col, -1)
-            staged[holder, edge:, :] = jnp.full((META_ROWS, width), code.astype(jnp.float32)).astype(staged.dtype)
-        pltpu.make_async_copy(values_ref.at[own], staged.at[own, pl.ds(0, edge)], read_sems.at[part]).wait()
+            staged[holder, pairs] = jnp.full((META_ROWS, width), code.astype(jnp.float32)).astype(staged.dtype)
+        pltpu.make_async_copy(values_ref.at[own], staged.at[own, pl.ds(0, pairs)], read_sems.at[part]).wait()
         pltpu.make_async_copy(staged.at[own], out_ref.at[own], write_sem).start()
     pltpu.make_async_copy(staged, out_ref, write_sem).wait()
 
 
 def pick_blocks(block_cols, block_rows, row_place, block_values):
     slots, edge, width = block_values.shape
-    out = (slots // 2, edge + META_ROWS, width)
+    pairs = edge // META_ROWS
+    out = (slots // 2, pairs + 1, META_ROWS, width)
     smem = pl.BlockSpec(memory_space=pltpu.SMEM)
     return pl.pallas_call(
         pick_kernel,
@@ -57,7 +59,7 @@
             pltpu.SemaphoreType.DMA((4,)),
             pltpu.SemaphoreType.DMA,
         ],
-    )(block_cols, block_rows, row_place, block_values)
+    )(block_cols, block_rows, row_place, block_values.reshape(slots, pairs, META_ROWS, width))
 
 
 def dense_part(vector, gram):
@@ -67,12 +69,15 @@
 
 def cg_kernel(
     blocks_ref, items, turned, gram, rest, factors, solution_ref, residual_ref,
-    weights, first_scores, meta, codes_vmem, codes, meta_sem, code_sem, block_sems,
+    weights, meta, codes_vmem, codes, meta_sem, code_sem, block_sems,
 ):
-    slots = blocks_ref.shape[0]
-    edge = blocks_ref.shape[1] - META_ROWS
+    slots, steps, _, width = blocks_ref.shape
+    edge = (steps - 1) * META_ROWS
+    blocks_ref = blocks_ref.reshape(slots, steps * META_ROWS, width)
     count = items.shape[0]
     panels = count // edge
+    shift = panels.bit_length() - 1
+    assert panels == 1 << shift
 
     meta_copy = pltpu.make_async_copy(blocks_ref.at[:, pl.ds(edge, META_ROWS)], meta, meta_sem)
     meta_copy.start()
@@ -85,8 +90,8 @@
 
     def block_copy(slot):
         code = codes[slot, 0]
-        user = pl.multiple_of((code // panels) * edge, edge)
-        item = pl.multiple_of((code % panels) * edge, edge)
+        user = pl.multiple_of(lax.shift_right_logical(code, shift) * edge, edge)
+        item = pl.multiple_of((code & (panels - 1)) * edge, edge)
         return pltpu.make_async_copy(
             blocks_ref.at[slot, pl.ds(0, edge)],
             weights.at[pl.ds(user, edge), pl.ds(item, edge)],
@@ -96,45 +101,54 @@
     for slot in range(slots):
         pl.when(codes[slot, 0] >= 0)(lambda slot=slot: block_copy(slot).start())
 
-    chunks = [slice(start, start + CHUNK) for start in range(0, count, CHUNK)]
-
-    def scores_of(direction, chunk):
-        return jnp.dot(direction, turned[:, chunk], preferred_element_type=jnp.float32)
-
-    for chunk in chunks:
-        first_scores[:, chunk] = scores_of(factors[...], chunk)
     for slot in range(slots):
         pl.when(codes[slot, 0] >= 0)(lambda slot=slot: block_copy(slot).wait())
 
-    block_sum = jnp.zeros(factors.shape, jnp.float32)
-    rhs = jnp.zeros(factors.shape, jnp.float32)
-    for chunk in chunks:
-        held = weights[:, chunk].astype(jnp.float32)
-        scaled = (first_scores[:, chunk] * held).astype(jnp.bfloat16)
-        block_sum += jnp.dot(scaled, items[chunk, :], preferred_element_type=jnp.float32)
-        confidence = jnp.where(held > 0, 1.0 + held, 0.0).astype(jnp.bfloat16)
-        rhs += jnp.dot(confidence, items[chunk, :], preferred_element_type=jnp.float32)
-
-    solution = factors[...].astype(jnp.float32)
-    residual = rhs - (block_sum + rest[...])
-    direction = residual
-    norm_now = jnp.sum(residual * residual, axis=1, keepdims=True)
+    chunks = [slice(start, start + CHUNK) for start in range(0, count, CHUNK)]
+    share = factors.shape[0] // PARTS
+    parts = [slice(part * share, (part + 1) * share) for part in range(PARTS)]
+
+    def scaled(rounded, held, chunk):
+        scores = jnp.dot(rounded, turned[:, chunk], preferred_element_type=jnp.float32)
+        return (scores * held).astype(jnp.bfloat16)
+
+    states = []
+    for part in parts:
+        block_sum = jnp.zeros((share, factors.shape[1]), jnp.float32)
+        rhs = block_sum
+        for chunk in chunks:
+            held = weights[part, chunk].astype(jnp.float32)
+            block_sum += jnp.dot(
+                scaled(factors[part, :], held, chunk), items[chunk, :], preferred_element_type=jnp.float32
+            )
+            confidence = jnp.where(held > 0, 1.0 + held, 0.0).astype(jnp.bfloat16)
+            rhs += jnp.dot(confidence, items[chunk, :], preferred_element_type=jnp.float32)
+        residual = rhs - (block_sum + rest[part, :])
+        norm_now = jnp.sum(residual * residual, axis=1, keepdims=True)
+        states.append((factors[part, :].astype(jnp.float32), residual, residual, norm_now))
+
     for sweep in range(ITERS):
-        rounded = direction.astype(jnp.bfloat16)
-        image = dense_part(direction, gram[...])
-        for chunk in chunks:
-            scaled = (scores_of(rounded, chunk) * weights[:, chunk].astype(jnp.float32)).astype(jnp.bfloat16)
-            image += jnp.dot(scaled, items[chunk, :], preferred_element_type=jnp.float32)
-        curvature = jnp.sum(direction * image, axis=1, keepdims=True)
-        step_length = norm_now / (curvature + epsilon)
-        solution = solution + step_length * direction
-        residual = residual - step_length * image
-        if sweep + 1 < ITERS:
-            norm_next = jnp.sum(residual * residual, axis=1, keepdims=True)
-            direction = residual + (norm_next / (norm_now + epsilon)) * direction
-            norm_now = norm_next
-    solution_ref[...] = solution
-    residual_ref[...] = residual
+        for index, part in enumerate(parts):
+            solution, residual, direction, norm_now = states[index]
+            rounded = direction.astype(jnp.bfloat16)
+            image = dense_part(direction, gram[...])
+            for chunk in chunks:
+                held = weights[part, chunk].astype(jnp.float32)
+                image += jnp.dot(
+                    scaled(rounded, held, chunk), items[chunk, :], preferred_element_type=jnp.float32
+                )
+            curvature = jnp.sum(direction * image, axis=1, keepdims=True)
+            step_length = norm_now / (curvature + epsilon)
+            solution = solution + step_length * direction
+            residual = residual - step_length * image
+            if sweep + 1 < ITERS:
+                norm_next = jnp.sum(residual * residual, axis=1, keepdims=True)
+                direction = residual + (norm_next / (norm_now + epsilon)) * direction
+                norm_now = norm_next
+                states[index] = (solution, residual, direction, norm_now)
+            else:
+                solution_ref[part, :] = solution
+                residual_ref[part, :] = residual
 
 
 def run_cg(blocks, items, turned, gram, first_rest, factors):
@@ -149,7 +163,6 @@
         out_specs=(vmem, vmem),
         scratch_shapes=[
             pltpu.VMEM((users, count), blocks.dtype),
-            pltpu.VMEM((users, count), jnp.float32),
             pltpu.VMEM((slots, META_ROWS, rank), blocks.dtype),
             pltpu.VMEM((slots, rank), jnp.int32),
             pltpu.SMEM((slots, rank), jnp.int32),

time: 89.9 us -> 85.7 us (0.953)
  waiting for transfers between devices: 23.4 us -> 21.1 us
  Pallas kernels: 12.4 us -> 10.6 us
    all_to_all x1, waiting for transfers between devices: 22.5 us -> 20.2 us  [body(): lax.all_to_all(picked, 'dev', split_axis=0, concat_axis=0, tiled=True)]
    pallas_call x1, Pallas kernels: 9.5 us -> 7.74 us  [run_cg(): pl.pallas_call(cg_kernel, out_shape=(out, out), in_specs=[pl.BlockSpec(me...]
where the time goes in v3:
time: 85.7 us; the launch traced here: 85.3 us
  starting transfers between devices  29 us (34%)
  blocking collectives  22.8 us (27%)
  waiting for transfers between devices  21.1 us (25%)
  Pallas kernels  10.6 us (12%)
    all_gather x1, blocking collectives, body(): lax.all_gather(pair, 'blk', axis=0, tiled=True, axis_index_groups=halves)  22.8 us
    all_to_all x1, waiting for transfers between devices, body(): lax.all_to_all(picked, 'dev', split_axis=0, concat_axis=0, tiled=True)  20.2 us
    all_to_all x1, starting transfers between devices, body(): lax.all_to_all(picked, 'dev', split_axis=0, concat_axis=0, tiled=True)  16.4 us
    ppermute x3, starting transfers between devices, from_other_group(): lax.ppermute(block, ('blk', 'dev'), border_pairs(group_count, dev_count,...  12.5 us
    pallas_call x1, Pallas kernels, run_cg(): pl.pallas_call(cg_kernel, out_shape=(out, out), in_specs=[pl.BlockSpec(me...  7.74 us
    pallas_call x1, Pallas kernels, pick_blocks(): pl.pallas_call(pick_kernel, out_shape=jax.ShapeDtypeStruct(out, block_val...  2.86 us
  transfers between devices with their start and end apart: 4, of which 2 were waited for; matrix products, arithmetic and copies ran while one was open for 1% of the time, Pallas kernels for 0%

profile of v3, /device:TPU:1, one launch (start us, length us, event | category | flops | bytes accessed | tf_op | source)
XLA Modules:
  0.0 85.3 jit_solution(14312622504218630907)
XLA Ops:
  0.6 2.9 %shard_map.77 = bf16[48,65,2,128]{3,2,1,0:T(2,128)(2,1)} custom-call(s32[96]{0:T(128)} %cols_ref.1, s32[96]{0:T(128)} %rows_ref.1, s32[1,192]{1,0:T(1,128)} %place_ref.1, bf16[96,64,2,128]{3,2,1,0:T(2,128)(2,1)} %bitcast.11), custom_call_target="tpu_custom_call" | custom-call | tf_op jit(solution)/shard_map/pallas_call | solution.py:52
  3.5 0.0 copy-start.1
  3.5 16.4 %all-to-all-start = ((bf16[48,65,2,128]{3,2,1,0:T(2,128)(2,1)}), bf16[48,65,2,128]{3,2,1,0:T(2,128)(2,1)S(1)}, u32[]{:S(2)}, u32[]{:S(2)}) async-start(bf16[48,65,2,128]{3,2,1,0:T(2,128)(2,1)} %shard_map.77), calls=%async_computation | async-start | bytes 3194880 | tf_op jit(solution)/shard_map/all_to_all | solution.py:211
  20.0 0.0 copy-done.1
  20.0 0.1 copy.11
  20.1 10.0 %collective-permute-start = (bf16[128,128]{0,1:T(8,128)(2,1)S(1)}, bf16[128,128]{0,1:T(8,128)(2,1)S(1)}, u32[]{:S(2)}, u32[]{:S(2)}) collective-permute-start(bf16[128,128]{0,1:T(8,128)(2,1)S(1)} %copy.11), channel_id=1, source_target_pairs={{0,58},{10,48},{1,59},{11,49},{12,70},{22,60},{13,71},{23,61},{24,... | collective-permute-start | bytes 98312 | tf_op jit(solution)/shard_map/ppermute | solution.py:200
  30.1 1.3 %collective-permute-start.1 = (bf16[128,128]{0,1:T(8,128)(2,1)S(1)}, bf16[128,128]{0,1:T(8,128)(2,1)S(1)}, u32[]{:S(2)}, u32[]{:S(2)}) collective-permute-start(bf16[128,128]{0,1:T(8,128)(2,1)S(1)} %copy.11), channel_id=1, source_target_pairs={{0,56},{10,50},{1,57},{11,51},{12,68},{22,62},{13,69},{23,63},{24,... | collective-permute-start | bytes 98312 | tf_op jit(solution)/shard_map/ppermute | solution.py:200
  31.4 1.3 %collective-permute-start.2 = (bf16[128,128]{0,1:T(8,128)(2,1)S(1)}, bf16[128,128]{0,1:T(8,128)(2,1)S(1)}, u32[]{:S(2)}, u32[]{:S(2)}) collective-permute-start(bf16[128,128]{0,1:T(8,128)(2,1)S(1)} %copy.11), channel_id=1, source_target_pairs={{0,54},{10,52},{1,55},{11,53},{12,66},{22,64},{13,67},{23,65},{24,... | collective-permute-start | bytes 98312 | tf_op jit(solution)/shard_map/ppermute | solution.py:200
  32.7 0.0 copy-start
  32.7 0.0 collective-permute-done
  32.7 0.0 collective-permute-done.1
  32.7 0.9 %collective-permute-done.2 = bf16[128,128]{0,1:T(8,128)(2,1)S(1)} collective-permute-done((bf16[128,128]{0,1:T(8,128)(2,1)S(1)}, bf16[128,128]{0,1:T(8,128)(2,1)S(1)}, u32[]{:S(2)}, u32[]{:S(2)}) %collective-permute-start.2) | collective-permute-done | bytes 32800 | tf_op jit(solution)/shard_map/ppermute | solution.py:200
  33.7 22.8 %all_gather.3 = bf16[2048,128]{0,1:T(8,128)(2,1)S(1)} all-gather(bf16[256,128]{0,1:T(8,128)(2,1)S(1)} %pad_maximum_fusion), channel_id=1, replica_groups={{0,96,192,288,384,480,576,672},{48,144,240,336,432,528,624,720},{1,97,1..., dimensions={0}, use_global_device_ids=true | all-gather | bytes 589824 | tf_op jit(solution)/shard_map/all_gather | solution.py:216
  56.5 0.3 copy.14.items
  56.8 0.3 fusion.1.gram
  57.1 0.0 copy-done
  57.1 0.3 fusion.rest
  57.4 20.2 %all-to-all-done.blocks_ref = bf16[48,65,2,128]{3,2,1,0:T(2,128)(2,1)S(1)} async-done(((bf16[48,65,2,128]{3,2,1,0:T(2,128)(2,1)}), bf16[48,65,2,128]{3,2,1,0:T(2,128)(2,1)S(1)}, u32[]{:S(2)}, u32[]{:S(2)}) %all-to-all-start) | async-done | bytes 1597472 | tf_op jit(solution)/shard_map/all_to_all | solution.py:211
  77.6 7.7 %shard_map.78 = (f32[512,128]{1,0:T(8,128)}, f32[512,128]{1,0:T(8,128)}) custom-call(bf16[48,65,2,128]{3,2,1,0:T(2,128)(2,1)S(1)} %all-to-all-done.blocks_ref, bf16[2048,128]{1,0:T(8,128)(2,1)S(1)} %copy.14.items, bf16[128,2048]{1,0:T(8,128)(2,1)S(1)} %bitcast.10, f32[128,128]{1,0:T(8,128)S(1)} %fusion.1.gram, f32[512,128]{1,0:T(8,128)S(1)} %fusion.rest, ...), custom_call_target="tpu_custom_call" | custom-call | tf_op jit(solution)/shard_map/pallas_call | solution.py:159
  (3 shorter events, 0.0 us)
Async XLA Ops:
  3.5 16.5 %copy-start.1 = (bf16[128,128]{1,0:T(8,128)(2,1)S(1)}, bf16[128,128]{1,0:T(8,128)(2,1)}, u32[]{:S(2)}) copy-start(bf16[128,128]{1,0:T(8,128)(2,1)} %param.7) | copy-start | bytes 98308
  3.5 74.1 %all-to-all-start = ((bf16[48,65,2,128]{3,2,1,0:T(2,128)(2,1)}), bf16[48,65,2,128]{3,2,1,0:T(2,128)(2,1)S(1)}, u32[]{:S(2)}, u32[]{:S(2)}) async-start(bf16[48,65,2,128]{3,2,1,0:T(2,128)(2,1)} %shard_map.77), calls=%async_computation | async-start | bytes 3194880 | tf_op jit(solution)/shard_map/all_to_all | solution.py:211
  20.1 12.6 %collective-permute-start = (bf16[128,128]{0,1:T(8,128)(2,1)S(1)}, bf16[128,128]{0,1:T(8,128)(2,1)S(1)}, u32[]{:S(2)}, u32[]{:S(2)}) collective-permute-start(bf16[128,128]{0,1:T(8,128)(2,1)S(1)} %copy.11), channel_id=1, source_target_pairs={{0,58},{10,48},{1,59},{11,49},{12,70},{22,60},{13,71},{23,61},{24,... | collective-permute-start | bytes 98312 | tf_op jit(solution)/shard_map/ppermute | solution.py:200
  30.1 2.7 %collective-permute-start.1 = (bf16[128,128]{0,1:T(8,128)(2,1)S(1)}, bf16[128,128]{0,1:T(8,128)(2,1)S(1)}, u32[]{:S(2)}, u32[]{:S(2)}) collective-permute-start(bf16[128,128]{0,1:T(8,128)(2,1)S(1)} %copy.11), channel_id=1, source_target_pairs={{0,56},{10,50},{1,57},{11,51},{12,68},{22,62},{13,69},{23,63},{24,... | collective-permute-start | bytes 98312 | tf_op jit(solution)/shard_map/ppermute | solution.py:200
  31.4 2.3 %collective-permute-start.2 = (bf16[128,128]{0,1:T(8,128)(2,1)S(1)}, bf16[128,128]{0,1:T(8,128)(2,1)S(1)}, u32[]{:S(2)}, u32[]{:S(2)}) collective-permute-start(bf16[128,128]{0,1:T(8,128)(2,1)S(1)} %copy.11), channel_id=1, source_target_pairs={{0,54},{10,52},{1,55},{11,53},{12,66},{22,64},{13,67},{23,65},{24,... | collective-permute-start | bytes 98312 | tf_op jit(solution)/shard_map/ppermute | solution.py:200
  32.7 24.4 %copy-start = (bf16[512,128]{1,0:T(8,128)(2,1)S(1)}, bf16[512,128]{1,0:T(8,128)(2,1)}, u32[]{:S(2)}) copy-start(bf16[512,128]{1,0:T(8,128)(2,1)} %factors.1) | copy-start | bytes 393220

commit v4 on v3

--- a/solution.py
+++ b/solution.py
@@ -56,7 +56,7 @@
         out_specs=pl.BlockSpec(memory_space=pl.ANY),
         scratch_shapes=[
             pltpu.VMEM(out, block_values.dtype),
-            pltpu.SemaphoreType.DMA((4,)),
+            pltpu.SemaphoreType.DMA((8,)),
             pltpu.SemaphoreType.DMA,
         ],
     )(block_cols, block_rows, row_place, block_values.reshape(slots, pairs, META_ROWS, width))
@@ -69,23 +69,21 @@
 
 def cg_kernel(
     blocks_ref, items, turned, gram, rest, factors, solution_ref, residual_ref,
-    weights, meta, codes_vmem, codes, meta_sem, code_sem, block_sems,
+    weights, codes_vmem, codes, code_sem, block_sems,
 ):
     slots, steps, _, width = blocks_ref.shape
     edge = (steps - 1) * META_ROWS
-    blocks_ref = blocks_ref.reshape(slots, steps * META_ROWS, width)
+    meta = blocks_ref[:, steps - 1]
+    blocks = blocks_ref.reshape(slots, steps * META_ROWS, width)
     count = items.shape[0]
     panels = count // edge
     shift = panels.bit_length() - 1
     assert panels == 1 << shift
 
-    meta_copy = pltpu.make_async_copy(blocks_ref.at[:, pl.ds(edge, META_ROWS)], meta, meta_sem)
-    meta_copy.start()
-    weights[...] = jnp.zeros_like(weights)
-    meta_copy.wait()
-    codes_vmem[...] = jnp.max(meta[...].astype(jnp.float32), axis=1).astype(jnp.int32)
+    codes_vmem[...] = jnp.max(meta.astype(jnp.float32), axis=1).astype(jnp.int32)
     code_copy = pltpu.make_async_copy(codes_vmem, codes, code_sem)
     code_copy.start()
+    weights[...] = jnp.zeros_like(weights)
     code_copy.wait()
 
     def block_copy(slot):
@@ -93,7 +91,7 @@
         user = pl.multiple_of(lax.shift_right_logical(code, shift) * edge, edge)
         item = pl.multiple_of((code & (panels - 1)) * edge, edge)
         return pltpu.make_async_copy(
-            blocks_ref.at[slot, pl.ds(0, edge)],
+            blocks.at[slot, pl.ds(0, edge)],
             weights.at[pl.ds(user, edge), pl.ds(item, edge)],
             block_sems.at[slot],
         )
@@ -159,14 +157,12 @@
     return pl.pallas_call(
         cg_kernel,
         out_shape=(out, out),
-        in_specs=[pl.BlockSpec(memory_space=pl.ANY)] + [vmem] * 5,
+        in_specs=[vmem] * 6,
         out_specs=(vmem, vmem),
         scratch_shapes=[
             pltpu.VMEM((users, count), blocks.dtype),
-            pltpu.VMEM((slots, META_ROWS, rank), blocks.dtype),
             pltpu.VMEM((slots, rank), jnp.int32),
             pltpu.SMEM((slots, rank), jnp.int32),
-            pltpu.SemaphoreType.DMA,
             pltpu.SemaphoreType.DMA,
             pltpu.SemaphoreType.DMA((slots,)),
         ],

time: 85.7 us -> 85.7 us (level)
  no operation moved by 1% of the time
where the time goes in v4:
time: 85.7 us; the launch traced here: 85.2 us
  starting transfers between devices  29 us (34%)
  blocking collectives  22.8 us (27%)
  waiting for transfers between devices  21.1 us (25%)
  Pallas kernels  10.5 us (12%)
    all_gather x1, blocking collectives, body(): lax.all_gather(pair, 'blk', axis=0, tiled=True, axis_index_groups=halves)  22.8 us
    all_to_all x1, waiting for transfers between devices, body(): lax.all_to_all(picked, 'dev', split_axis=0, concat_axis=0, tiled=True)  20.2 us
    all_to_all x1, starting transfers between devices, body(): lax.all_to_all(picked, 'dev', split_axis=0, concat_axis=0, tiled=True)  16.4 us
    ppermute x3, starting transfers between devices, from_other_group(): lax.ppermute(block, ('blk', 'dev'), border_pairs(group_count, dev_count,...  12.5 us
    pallas_call x1, Pallas kernels, run_cg(): pl.pallas_call(cg_kernel, out_shape=(out, out), in_specs=[vmem] * 6, out_...  7.67 us
    pallas_call x1, Pallas kernels, pick_blocks(): pl.pallas_call(pick_kernel, out_shape=jax.ShapeDtypeStruct(out, block_val...  2.84 us
  transfers between devices with their start and end apart: 4, of which 2 were waited for; matrix products, arithmetic and copies ran while one was open for 1% of the time, Pallas kernels for 0%

profile of v4, /device:TPU:1, one launch (start us, length us, event | category | flops | bytes accessed | tf_op | source)
XLA Modules:
  0.0 85.2 jit_solution(13655053531247320155)
XLA Ops:
  0.6 2.8 %shard_map.77 = bf16[48,65,2,128]{3,2,1,0:T(2,128)(2,1)} custom-call(s32[96]{0:T(128)} %cols_ref.1, s32[96]{0:T(128)} %rows_ref.1, s32[1,192]{1,0:T(1,128)} %place_ref.1, bf16[96,64,2,128]{3,2,1,0:T(2,128)(2,1)} %bitcast.11), custom_call_target="tpu_custom_call" | custom-call | tf_op jit(solution)/shard_map/pallas_call | solution.py:52
  3.5 0.0 copy-start.1
  3.5 16.4 %all-to-all-start = ((bf16[48,65,2,128]{3,2,1,0:T(2,128)(2,1)}), bf16[48,65,2,128]{3,2,1,0:T(2,128)(2,1)S(1)}, u32[]{:S(2)}, u32[]{:S(2)}) async-start(bf16[48,65,2,128]{3,2,1,0:T(2,128)(2,1)} %shard_map.77), calls=%async_computation | async-start | bytes 3194880 | tf_op jit(solution)/shard_map/all_to_all | solution.py:207
  19.9 0.0 copy-done.1
  19.9 0.1 copy.11
  20.1 10.0 %collective-permute-start = (bf16[128,128]{0,1:T(8,128)(2,1)S(1)}, bf16[128,128]{0,1:T(8,128)(2,1)S(1)}, u32[]{:S(2)}, u32[]{:S(2)}) collective-permute-start(bf16[128,128]{0,1:T(8,128)(2,1)S(1)} %copy.11), channel_id=1, source_target_pairs={{0,58},{10,48},{1,59},{11,49},{12,70},{22,60},{13,71},{23,61},{24,... | collective-permute-start | bytes 98312 | tf_op jit(solution)/shard_map/ppermute | solution.py:196
  30.0 1.3 %collective-permute-start.1 = (bf16[128,128]{0,1:T(8,128)(2,1)S(1)}, bf16[128,128]{0,1:T(8,128)(2,1)S(1)}, u32[]{:S(2)}, u32[]{:S(2)}) collective-permute-start(bf16[128,128]{0,1:T(8,128)(2,1)S(1)} %copy.11), channel_id=1, source_target_pairs={{0,56},{10,50},{1,57},{11,51},{12,68},{22,62},{13,69},{23,63},{24,... | collective-permute-start | bytes 98312 | tf_op jit(solution)/shard_map/ppermute | solution.py:196
  31.3 1.3 %collective-permute-start.2 = (bf16[128,128]{0,1:T(8,128)(2,1)S(1)}, bf16[128,128]{0,1:T(8,128)(2,1)S(1)}, u32[]{:S(2)}, u32[]{:S(2)}) collective-permute-start(bf16[128,128]{0,1:T(8,128)(2,1)S(1)} %copy.11), channel_id=1, source_target_pairs={{0,54},{10,52},{1,55},{11,53},{12,66},{22,64},{13,67},{23,65},{24,... | collective-permute-start | bytes 98312 | tf_op jit(solution)/shard_map/ppermute | solution.py:196
  32.7 0.0 copy-start
  32.7 0.0 collective-permute-done
  32.7 0.0 collective-permute-done.1
  32.7 0.9 %collective-permute-done.2 = bf16[128,128]{0,1:T(8,128)(2,1)S(1)} collective-permute-done((bf16[128,128]{0,1:T(8,128)(2,1)S(1)}, bf16[128,128]{0,1:T(8,128)(2,1)S(1)}, u32[]{:S(2)}, u32[]{:S(2)}) %collective-permute-start.2) | collective-permute-done | bytes 32800 | tf_op jit(solution)/shard_map/ppermute | solution.py:196
  33.7 22.8 %all_gather.3 = bf16[2048,128]{0,1:T(8,128)(2,1)S(1)} all-gather(bf16[256,128]{0,1:T(8,128)(2,1)S(1)} %pad_maximum_fusion), channel_id=1, replica_groups={{0,96,192,288,384,480,576,672},{48,144,240,336,432,528,624,720},{1,97,1..., dimensions={0}, use_global_device_ids=true | all-gather | bytes 589824 | tf_op jit(solution)/shard_map/all_gather | solution.py:212
  56.5 0.3 copy.14.items
  56.8 0.3 fusion.1.gram
  57.1 0.0 copy-done
  57.1 0.3 fusion.rest
  57.4 20.2 %all-to-all-done.blocks_ref = bf16[48,65,2,128]{3,2,1,0:T(2,128)(2,1)S(1)} async-done(((bf16[48,65,2,128]{3,2,1,0:T(2,128)(2,1)}), bf16[48,65,2,128]{3,2,1,0:T(2,128)(2,1)S(1)}, u32[]{:S(2)}, u32[]{:S(2)}) %all-to-all-start) | async-done | bytes 1597472 | tf_op jit(solution)/shard_map/all_to_all | solution.py:207
  77.6 7.7 %shard_map.78 = (f32[512,128]{1,0:T(8,128)}, f32[512,128]{1,0:T(8,128)}) custom-call(bf16[48,65,2,128]{3,2,1,0:T(2,128)(2,1)S(1)} %all-to-all-done.blocks_ref, bf16[2048,128]{1,0:T(8,128)(2,1)S(1)} %copy.14.items, bf16[128,2048]{1,0:T(8,128)(2,1)S(1)} %bitcast.10, f32[128,128]{1,0:T(8,128)S(1)} %fusion.1.gram, f32[512,128]{1,0:T(8,128)S(1)} %fusion.rest, ...), custom_call_target="tpu_custom_call" | custom-call | tf_op jit(solution)/shard_map/pallas_call | solution.py:157
  (3 shorter events, 0.0 us)
Async XLA Ops:
  3.5 16.5 %copy-start.1 = (bf16[128,128]{1,0:T(8,128)(2,1)S(1)}, bf16[128,128]{1,0:T(8,128)(2,1)}, u32[]{:S(2)}) copy-start(bf16[128,128]{1,0:T(8,128)(2,1)} %param.7) | copy-start | bytes 98308
  3.5 74.1 %all-to-all-start = ((bf16[48,65,2,128]{3,2,1,0:T(2,128)(2,1)}), bf16[48,65,2,128]{3,2,1,0:T(2,128)(2,1)S(1)}, u32[]{:S(2)}, u32[]{:S(2)}) async-start(bf16[48,65,2,128]{3,2,1,0:T(2,128)(2,1)} %shard_map.77), calls=%async_computation | async-start | bytes 3194880 | tf_op jit(solution)/shard_map/all_to_all | solution.py:207
  20.1 12.6 %collective-permute-start = (bf16[128,128]{0,1:T(8,128)(2,1)S(1)}, bf16[128,128]{0,1:T(8,128)(2,1)S(1)}, u32[]{:S(2)}, u32[]{:S(2)}) collective-permute-start(bf16[128,128]{0,1:T(8,128)(2,1)S(1)} %copy.11), channel_id=1, source_target_pairs={{0,58},{10,48},{1,59},{11,49},{12,70},{22,60},{13,71},{23,61},{24,... | collective-permute-start | bytes 98312 | tf_op jit(solution)/shard_map/ppermute | solution.py:196
  30.0 2.7 %collective-permute-start.1 = (bf16[128,128]{0,1:T(8,128)(2,1)S(1)}, bf16[128,128]{0,1:T(8,128)(2,1)S(1)}, u32[]{:S(2)}, u32[]{:S(2)}) collective-permute-start(bf16[128,128]{0,1:T(8,128)(2,1)S(1)} %copy.11), channel_id=1, source_target_pairs={{0,56},{10,50},{1,57},{11,51},{12,68},{22,62},{13,69},{23,63},{24,... | collective-permute-start | bytes 98312 | tf_op jit(solution)/shard_map/ppermute | solution.py:196
  31.3 2.3 %collective-permute-start.2 = (bf16[128,128]{0,1:T(8,128)(2,1)S(1)}, bf16[128,128]{0,1:T(8,128)(2,1)S(1)}, u32[]{:S(2)}, u32[]{:S(2)}) collective-permute-start(bf16[128,128]{0,1:T(8,128)(2,1)S(1)} %copy.11), channel_id=1, source_target_pairs={{0,54},{10,52},{1,55},{11,53},{12,66},{22,64},{13,67},{23,65},{24,... | collective-permute-start | bytes 98312 | tf_op jit(solution)/shard_map/ppermute | solution.py:196
  32.7 24.4 %copy-start = (bf16[512,128]{1,0:T(8,128)(2,1)S(1)}, bf16[512,128]{1,0:T(8,128)(2,1)}, u32[]{:S(2)}) copy-start(bf16[512,128]{1,0:T(8,128)(2,1)} %factors.1) | copy-start | bytes 393220
